TPU v7x, 32 devices: a whole 2x2x4 slice. The times are simulated.
32 devices in a mesh: tile: 8 (over z, y), hidden: 4 (over x, core).
Axes of the slice: x: 2, y: 2, z: 4, core: 2. Of those that a mesh axis runs over, the one named last changes fastest.
Arguments:
- cells: bfloat16 [128, 48, 48, 128], P(('tile', 'hidden')), may hold values from -6 to 6
- partner_edge: int32 [128, 4], P(('tile', 'hidden')), may hold values from 0 to 511, as said below
- edge_flip: int32 [128, 4], P(('tile', 'hidden')), may hold values from 0 to 1, as said below
- dw_weight: float32 [9, 128], replicated, may hold values from -2 to 2
- dw_bias: float32 [128], replicated, may hold values from -3 to 3
- ln_gain: float32 [128], replicated, may hold values from 0.5 to 1.5
- ln_bias: float32 [128], replicated, may hold values from -3 to 3
- w_in: bfloat16 [512, 128], replicated, may hold values from -0.5 to 0.5
- b_in: bfloat16 [512], replicated, may hold values from -3 to 3
- w_out: bfloat16 [512, 128], replicated, may hold values from -0.25 to 0.25
- b_out: float32 [128], replicated, may hold values from -3 to 3
- layer_scale: float32 [128], replicated, may hold values from 0.5 to 1.5
Outputs:
- updated: bfloat16 [128, 48, 48, 128], P(('tile', 'hidden'))
Inputs may be any that keep to these rules, and one draw needn't show every extreme that they name: `partner_edge`: edges are matched in pairs: if edge a names edge b, then b names a, a != b, and both carry the same edge_flip. Every edge's partner lies on the same device as its tile or on the device just before or just after it in the order of tile+hidden, the last and the first being neighbours; exactly 4 edges of each device have partners on the next device. `edge_flip`: equal at the two edges of a matched pair.
All inputs are finite; a program needn't handle non-finite values.
Results may differ from a plain program's by a relative error of at most 0.0044.
Values may be sent and summed in bfloat16 or wider, within the bound.
A program may use at most 64 MiB of HBM per device.

v0:
```python
import functools

import jax
import jax.numpy as jnp
from jax import lax
from jax.experimental import pallas as pl
from jax.experimental.pallas import tpu as pltpu
from jax.sharding import PartitionSpec as P

AXES = ("tile", "hidden")
OFF = 8
ROWS = 8
UNROLL = 2
CROSS = 4
GRANT = 40 * 1024 * 1024
MESH = pl.DeviceIdType.MESH
ROOT_HALF = 0.7071067811865476


def tile_of(q, per_tile, tiles):
    tile = 0
    for j in range(1, tiles):
        tile = tile + jnp.where(q >= j * per_tile, 1, 0)
    return tile


def row_lines(pad_ref, side, tile, row):
    line = tile * (side + 2) + row
    return lambda a, b: pad_ref[line + a, pl.ds(OFF - 1 + b, side), :]


def col_lines(flat_pad, side, width, tile, col):
    first = tile * (side + 2) * width + OFF - 1 + col
    return lambda a, b: flat_pad[pl.ds(first + a * width + b, side, stride=width), :]


def conv(dw_ref, dw_bias_ref, side, segments, dst):
    channels = dw_ref.shape[1]
    for n, load in enumerate(segments):
        total = jnp.broadcast_to(dw_bias_ref[...], (side, channels))
        for a in range(3):
            for b in range(3):
                total = total + dw_ref[3 * a + b : 3 * a + b + 1] * load(a, b)
        center = total - jnp.mean(total, axis=-1, keepdims=True)
        spread = jnp.sum(center * center, axis=-1, keepdims=True)
        value = center * lax.rsqrt(spread + 1e-06 * channels)
        dst[n * side : (n + 1) * side, 0:channels] = value.astype(jnp.bfloat16)


def mlp(w_aug_ref, w_fin_ref, bias_ref, side, segments, src):
    z = jnp.dot(src[...], w_aug_ref[...], preferred_element_type=jnp.float32)
    z = z.astype(jnp.bfloat16)
    act = z * (lax.erf(z) + jnp.bfloat16(1))
    mixed = jnp.dot(act, w_fin_ref[...], preferred_element_type=jnp.float32)
    for n, (load, store) in enumerate(segments):
        store(load(1, 1) + (mixed[n * side : (n + 1) * side] + bias_ref[...]))


def fill_ones(buf):
    rows, both = buf.shape
    lane = lax.broadcasted_iota(jnp.int32, (rows, both // 2), 1)
    buf[:, both // 2 :] = jnp.where(lane < 2, 1.0, 0.0).astype(jnp.bfloat16)


def last_flagged(flags, values):
    found = [jnp.int32(0)] * CROSS
    for flag, value in zip(flags, values):
        for k in range(CROSS - 1, 0, -1):
            found[k] = jnp.where(flag, found[k - 1], found[k])
        found[0] = jnp.where(flag, value, found[0])
    return found


def owned(partner, device, edges):
    local = partner - device * edges
    return (local >= 0) & (local < edges), local


def above(values, limit):
    return sum(jnp.where(value > limit, 1, 0) for value in values)


def split_bf16(value):
    high = value.astype(jnp.bfloat16).astype(jnp.float32)
    return high, value - high


def fold_weights(gain_ref, ln_bias_ref, w_in, b_in, w_out, b_out_ref, scale_ref, w_aug_ref, w_fin_ref, bias_ref):
    hidden, channels = w_in.shape
    eye = (
        lax.broadcasted_iota(jnp.int32, (channels, channels), 0)
        == lax.broadcasted_iota(jnp.int32, (channels, channels), 1)
    ).astype(jnp.bfloat16)
    gain = gain_ref[...] * (ROOT_HALF * channels**0.5)
    w_gain = (w_in.astype(jnp.float32) * gain).astype(jnp.bfloat16)
    turned = (((1,), (1,)), ((), ()))
    w_aug_ref[0:channels, :] = lax.dot_general(
        eye, w_gain, turned, preferred_element_type=jnp.float32
    ).astype(jnp.bfloat16)
    high, rest = split_bf16(ln_bias_ref[...])
    middle, low = split_bf16(rest)
    row_id = lax.broadcasted_iota(jnp.int32, (16, channels), 0)
    parts = jnp.where(
        row_id == 0, high, jnp.where(row_id == 1, middle, jnp.where(row_id == 2, low, 0.0))
    ).astype(jnp.bfloat16)
    moved = lax.dot_general(parts, w_in, turned, preferred_element_type=jnp.float32)
    moved = jnp.sum(moved, axis=0, keepdims=True)
    total = (b_in.astype(jnp.float32).reshape(1, hidden) + moved) * ROOT_HALF
    high, rest = split_bf16(total)
    row_id = lax.broadcasted_iota(jnp.int32, (channels, hidden), 0)
    extra = jnp.where(row_id == 0, high, jnp.where(row_id == 1, rest, 0.0))
    w_aug_ref[channels : 2 * channels, :] = extra.astype(jnp.bfloat16)
    scale = scale_ref[...]
    w_fin_ref[...] = (w_out.astype(jnp.float32) * (scale * ROOT_HALF)).astype(jnp.bfloat16)
    bias_ref[...] = scale * b_out_ref[...]


def inner_kernel(
    sizes,
    cells_ref,
    partner_hbm,
    flip_hbm,
    dw_hbm,
    dw_bias_hbm,
    gain_hbm,
    ln_bias_hbm,
    w_in_hbm,
    b_in_hbm,
    w_out_hbm,
    b_out_hbm,
    scale_hbm,
    mid_ref,
    strip_ref,
    pad_ref,
    w_aug_ref,
    w_fin_ref,
    dw_ref,
    dw_bias_ref,
    bias_ref,
    cells_buf,
    rims_ref,
    recv_ref,
    send_buf,
    buf_a,
    buf_b,
    partner_ref,
    flip_ref,
    gain_ref,
    ln_bias_ref,
    w_in_ref,
    b_in_ref,
    w_out_ref,
    b_out_ref,
    scale_ref,
    load_sem,
    table_sem,
    weight_sem,
    send_sem,
    recv_sem,
):
    tile_devices, hidden_devices = sizes
    tiles, side, _, channels = cells_buf.shape
    edges = 4 * tiles
    width = side + 2 * OFF
    devices = tile_devices * hidden_devices
    me = lax.axis_index("tile") * hidden_devices + lax.axis_index("hidden")

    def at(position):
        return (position // hidden_devices, position % hidden_devices)

    right = lax.rem(me + 1, devices)
    left = lax.rem(me + devices - 1, devices)
    loads = [
        pltpu.make_async_copy(cells_ref.at[t], cells_buf.at[t], load_sem.at[t])
        for t in range(tiles)
    ]
    tables = [
        pltpu.make_async_copy(src, dst, table_sem.at[n])
        for n, (src, dst) in enumerate(((partner_hbm, partner_ref), (flip_hbm, flip_ref)))
    ]
    weights = [
        pltpu.make_async_copy(src, dst, weight_sem.at[n])
        for n, (src, dst) in enumerate(
            (
                (w_in_hbm, w_in_ref),
                (w_out_hbm, w_out_ref),
                (b_in_hbm, b_in_ref),
                (gain_hbm, gain_ref),
                (ln_bias_hbm, ln_bias_ref),
                (b_out_hbm, b_out_ref),
                (scale_hbm, scale_ref),
                (dw_hbm, dw_ref),
                (dw_bias_hbm, dw_bias_ref),
            )
        )
    ]
    for copy in tables + weights[:3] + loads[:1] + weights[3:] + loads[1:]:
        copy.start()
    barrier = pltpu.get_barrier_semaphore()
    for neighbour in (left, right):
        pl.semaphore_signal(barrier, inc=1, device_id=at(neighbour), device_id_type=MESH)

    fill_ones(buf_a)
    fill_ones(buf_b)
    for copy in weights:
        copy.wait()
    fold_weights(
        gain_ref,
        ln_bias_ref,
        w_in_ref[...],
        b_in_ref[...],
        w_out_ref[...],
        b_out_ref,
        scale_ref,
        w_aug_ref,
        w_fin_ref,
        bias_ref,
    )
    for copy in tables:
        copy.wait()
    partners = [partner_ref[e // 4, e % 4] for e in range(edges)]
    local = [jnp.int32(e) for e in range(edges)]
    going = []
    for device in (right, left):
        going += last_flagged([owned(p, device, edges)[0] for p in partners], local)

    flat_pad = pad_ref.reshape(tiles * (side + 2) * width, channels)
    for t in range(tiles):
        loads[t].wait()
        top = t * (side + 2)
        pad_ref[pl.ds(top + 1, side), pl.ds(OFF, side), :] = cells_buf[t].astype(jnp.float32)
        first = (top + 1) * width + OFF
        mine = 4 * t
        rims_ref[mine] = cells_buf[t, 0]
        rims_ref[mine + 2] = cells_buf[t, side - 1]
        east = flat_pad[pl.ds(first + side - 1, side, stride=width), :]
        rims_ref[mine + 1] = east.astype(jnp.bfloat16)
        west = flat_pad[pl.ds(first, side, stride=width), :]
        rims_ref[mine + 3] = west.astype(jnp.bfloat16)
    for k in range(2 * CROSS):
        send_buf[k] = rims_ref[going[k]]

    sends = [
        pltpu.make_async_remote_copy(
            src_ref=send_buf.at[pl.ds(side_id * CROSS, CROSS)],
            dst_ref=recv_ref.at[pl.ds(side_id * CROSS, CROSS)],
            send_sem=send_sem.at[side_id],
            recv_sem=recv_sem.at[side_id],
            device_id=at(target),
            device_id_type=MESH,
        )
        for side_id, target in ((0, right), (1, left))
    ]

    def send():
        pl.semaphore_wait(barrier, 2)
        for copy in sends:
            copy.start()

    inner_rows = side - 2

    def rows_of(chunk):
        found = []
        for k in range(ROWS):
            q = chunk * ROWS + k
            tile = tile_of(q, inner_rows, tiles)
            found.append((tile, q - inner_rows * tile + 1))
        return found

    def do_conv(chunk, dst):
        lines = [row_lines(pad_ref, side, tile, row) for tile, row in rows_of(chunk)]
        conv(dw_ref, dw_bias_ref, side, lines, dst)

    def put(tile, row):
        def store(new):
            mid_ref[tile, row] = new[OFF : side - OFF].astype(jnp.bfloat16)
            strip_ref[tile, row, 0:OFF, :] = new[:OFF]
            strip_ref[tile, row, OFF:, :] = new[side - OFF :]

        return store

    def do_mlp(chunk, src):
        lines = [
            (row_lines(pad_ref, side, tile, row), put(tile, row)) for tile, row in rows_of(chunk)
        ]
        mlp(w_aug_ref, w_fin_ref, bias_ref, side, lines, src)

    chunks = tiles * inner_rows // ROWS
    bufs = (buf_a, buf_b)
    do_conv(0, buf_a)
    rounds = (chunks - 1) // UNROLL
    turn = jnp.where(me == 0, rounds - 1, jnp.where(me == devices - 1, 0, min(2, rounds - 1)))

    @pl.loop(0, rounds)
    def _(i):
        @pl.when(i == turn)
        def _():
            send()

        for u in range(UNROLL):
            do_mlp(UNROLL * i + u, bufs[u % 2])
            do_conv(UNROLL * i + u + 1, bufs[(u + 1) % 2])

    for c in range((chunks - 1) // UNROLL * UNROLL, chunks):
        do_mlp(c, bufs[c % 2])
        if c + 1 < chunks:
            do_conv(c + 1, bufs[(c + 1) % 2])
    for copy in sends:
        copy.wait()

    prev_flags, prev_local = zip(*[owned(p, left, edges) for p in partners])
    next_flags, next_local = zip(*[owned(p, right, edges) for p in partners])
    prev_list = last_flagged(prev_flags, prev_local)
    next_list = last_flagged(next_flags, next_local)
    r_id = lax.broadcasted_iota(jnp.int32, (side, side), 0)
    c_id = lax.broadcasted_iota(jnp.int32, (side, side), 1)
    for t in range(tiles):
        lines = []
        for s in range(4):
            e = 4 * t + s
            is_prev, is_next = prev_flags[e], next_flags[e]
            slot = jnp.where(
                is_prev,
                above(prev_list, prev_local[e]),
                CROSS + above(next_list, next_local[e]),
            )
            crosses = is_prev | is_next
            own_edge = jnp.clip(jnp.where(crosses, 0, partners[e] - me * edges), 0, edges - 1)
            received = recv_ref[jnp.clip(jnp.where(crosses, slot, 0), 0, 2 * CROSS - 1)]
            line = jnp.where(crosses, received, rims_ref[own_edge])
            target = jnp.where(flip_ref[t, s] == 1, side - 1 - r_id, r_id)
            order = jnp.where(c_id == target, 1.0, 0.0).astype(jnp.bfloat16)
            lines.append(jnp.dot(order, line, preferred_element_type=jnp.float32))
        north, east, south, west = lines
        top = t * (side + 2)
        end = top + side + 1
        pad_ref[top, pl.ds(OFF, side), :] = north
        pad_ref[end, pl.ds(OFF, side), :] = south
        first = (top + 1) * width + OFF
        flat_pad[pl.ds(first - 1, side, stride=width), :] = west
        flat_pad[pl.ds(first + side, side, stride=width), :] = east
        pad_ref[top, OFF - 1 : OFF, :] = 0.5 * (north[:1] + west[:1])
        pad_ref[top, OFF + side : OFF + side + 1, :] = 0.5 * (north[-1:] + east[:1])
        pad_ref[end, OFF - 1 : OFF, :] = 0.5 * (south[:1] + west[-1:])
        pad_ref[end, OFF + side : OFF + side + 1, :] = 0.5 * (south[-1:] + east[-1:])


def edge_kernel(
    mid_ref,
    strip_in_ref,
    pad_ref,
    w_aug_ref,
    w_fin_ref,
    dw_ref,
    dw_bias_ref,
    bias_ref,
    out_hbm,
    strip_ref,
    caps_ref,
    sides_ref,
    buf_a,
    buf_b,
    mid_sem,
    cap_sem,
    side_sem,
):
    tiles, side, _, channels = out_hbm.shape
    width = side + 2 * OFF
    mid_copies = [
        pltpu.make_async_copy(
            mid_ref.at[t, pl.ds(1, side - 2)],
            out_hbm.at[t, pl.ds(1, side - 2), pl.ds(OFF, side - 2 * OFF)],
            mid_sem.at[t],
        )
        for t in range(tiles)
    ]
    for copy in mid_copies:
        copy.start()
    fill_ones(buf_a)
    fill_ones(buf_b)
    flat_pad = pad_ref.reshape(tiles * (side + 2) * width, channels)
    flat_strip = strip_ref.reshape(tiles * side * 2 * OFF, channels)

    def put_cap(tile, n):
        def store(new):
            caps_ref[tile, n] = new.astype(jnp.bfloat16)

        return store

    def put_side(tile, n):
        first = tile * side * 2 * OFF + n * (2 * OFF - 1)

        def store(new):
            flat_strip[pl.ds(first, side, stride=2 * OFF), :] = new

        return store

    def lines_of(tile):
        return [
            (row_lines(pad_ref, side, tile, 0), put_cap(tile, 0)),
            (row_lines(pad_ref, side, tile, side - 1), put_cap(tile, 1)),
            (col_lines(flat_pad, side, width, tile, 0), put_side(tile, 0)),
            (col_lines(flat_pad, side, width, tile, side - 1), put_side(tile, 1)),
        ]

    groups = [
        [line for t in range(g, g + 2) for line in lines_of(t)] for g in range(0, tiles, 2)
    ]
    bufs = (buf_a, buf_b)
    copies = []

    def finish(g):
        for t in (2 * g, 2 * g + 1):
            for n, row in enumerate((0, side - 1)):
                copies.append(
                    pltpu.make_async_copy(
                        caps_ref.at[t, n], out_hbm.at[t, row], cap_sem.at[t, n]
                    )
                )
                copies[-1].start()
            for n, col in enumerate((0, side - OFF)):
                sides_ref[t, n] = strip_ref[t, :, n * OFF : (n + 1) * OFF, :].astype(jnp.bfloat16)
                copies.append(
                    pltpu.make_async_copy(
                        sides_ref.at[t, n, pl.ds(1, side - 2)],
                        out_hbm.at[t, pl.ds(1, side - 2), pl.ds(col, OFF)],
                        side_sem.at[t, n],
                    )
                )
                copies[-1].start()

    for g, group in enumerate(groups):
        conv(dw_ref, dw_bias_ref, side, [load for load, _ in group], bufs[g % 2])
        if g:
            mlp(w_aug_ref, w_fin_ref, bias_ref, side, groups[g - 1], bufs[(g - 1) % 2])
            finish(g - 1)
    mlp(w_aug_ref, w_fin_ref, bias_ref, side, groups[-1], bufs[(len(groups) - 1) % 2])
    finish(len(groups) - 1)
    for copy in mid_copies + copies:
        copy.wait()


def per_device(sizes, cells, *rest):
    tables, (dw_weight, dw_bias, ln_gain, ln_bias, w_in, b_in, w_out, b_out, layer_scale) = (
        rest[:2],
        rest[2:],
    )
    tiles, side, _, channels = cells.shape
    hidden = w_in.shape[0]
    edges = 4 * tiles
    vmem = pl.BlockSpec(memory_space=pltpu.VMEM)
    anywhere = pl.BlockSpec(memory_space=pltpu.HBM)
    dw_bias, ln_gain, ln_bias, b_out, layer_scale = (
        vector.reshape(1, channels)
        for vector in (dw_bias, ln_gain, ln_bias, b_out, layer_scale)
    )
    operands = [
        pltpu.with_memory_space_constraint(array, pltpu.HBM)
        for array in (
            cells,
            *tables,
            dw_weight,
            dw_bias,
            ln_gain,
            ln_bias,
            w_in,
            b_in,
            w_out,
            b_out,
            layer_scale,
        )
    ]
    pad_shape = (tiles * (side + 2), side + 2 * OFF, channels)
    strip_shape = (tiles, side, 2 * OFF, channels)
    vector = pltpu.VMEM((1, channels), jnp.float32)
    buffers = [pltpu.VMEM((ROWS * side, 2 * channels), jnp.bfloat16)] * 2
    passed = pl.pallas_call(
        functools.partial(inner_kernel, sizes),
        out_shape=(
            pltpu.VMEM((tiles, side, side - 2 * OFF, channels), jnp.bfloat16),
            pltpu.VMEM(strip_shape, jnp.float32),
            pltpu.VMEM(pad_shape, jnp.float32),
            pltpu.VMEM((2 * channels, hidden), jnp.bfloat16),
            pltpu.VMEM((hidden, channels), jnp.bfloat16),
            pltpu.VMEM(dw_weight.shape, jnp.float32),
            vector,
            vector,
        ),
        in_specs=[anywhere] * len(operands),
        out_specs=(vmem,) * 8,
        scratch_shapes=[
            pltpu.VMEM(cells.shape, jnp.bfloat16),
            pltpu.VMEM((edges, side, channels), jnp.bfloat16),
            pltpu.VMEM((2 * CROSS, side, channels), jnp.bfloat16),
            pltpu.VMEM((2 * CROSS, side, channels), jnp.bfloat16),
            *buffers,
            pltpu.SMEM(tables[0].shape, jnp.int32),
            pltpu.SMEM(tables[1].shape, jnp.int32),
            vector,
            vector,
            pltpu.VMEM(w_in.shape, jnp.bfloat16),
            pltpu.VMEM(b_in.shape, jnp.bfloat16),
            pltpu.VMEM(w_out.shape, jnp.bfloat16),
            vector,
            vector,
            pltpu.SemaphoreType.DMA((tiles,)),
            pltpu.SemaphoreType.DMA((2,)),
            pltpu.SemaphoreType.DMA((9,)),
            pltpu.SemaphoreType.DMA((2,)),
            pltpu.SemaphoreType.DMA((2,)),
        ],
        compiler_params=pltpu.CompilerParams(
            collective_id=0, has_side_effects=True, vmem_limit_bytes=GRANT
        ),
        name="inner",
    )(*operands)
    return pl.pallas_call(
        edge_kernel,
        out_shape=(
            jax.ShapeDtypeStruct(cells.shape, jnp.bfloat16),
            pltpu.VMEM(strip_shape, jnp.float32),
        ),
        in_specs=[vmem] * 8,
        out_specs=(anywhere, vmem),
        input_output_aliases={1: 1},
        scratch_shapes=[
            pltpu.VMEM((tiles, 2, side, channels), jnp.bfloat16),
            pltpu.VMEM((tiles, 2, side, OFF, channels), jnp.bfloat16),
            *buffers,
            pltpu.SemaphoreType.DMA((tiles,)),
            pltpu.SemaphoreType.DMA((tiles, 2)),
            pltpu.SemaphoreType.DMA((tiles, 2)),
        ],
        compiler_params=pltpu.CompilerParams(vmem_limit_bytes=GRANT),
        name="edge",
    )(*passed)[0]


def solution(mesh):
    spread_spec = P(AXES, None, None, None)
    in_specs = (spread_spec, P(AXES, None), P(AXES, None)) + (P(),) * 9
    sizes = (mesh.shape["tile"], mesh.shape["hidden"])
    return jax.shard_map(
        functools.partial(per_device, sizes),
        mesh=mesh,
        in_specs=in_specs,
        out_specs=spread_spec,
        check_vma=False,
    )
```

profile of v0, /device:TPU:0, one launch (start us, length us, event | category | flops | bytes accessed | tf_op | source)
XLA Modules:
  0.0 15.0 jit_solution(8935014132000733402)
XLA Ops:
  0.0 12.3 %inner.1 = (bf16[4,48,32,128]{3,2,1,0:T(8,128)(2,1)S(1)}, f32[4,48,16,128]{3,2,1,0:T(8,128)S(1)}, f32[200,64,128]{2,1,0:T(8,128)S(1)}, bf16[256,512]{1,0:T(8,128...) custom-call(bf16[4,48,48,128]{3,2,1,0:T(8,128)(2,1)} %cells_ref.1, ...), custom_call_target="tpu_custom_call" | custom-call | tf_op jit(solution)/shard_map/inner/pallas_call | solution.py:477
  12.3 2.7 %edge.1 = (bf16[4,48,48,128]{3,2,1,0:T(8,128)(2,1)}, f32[4,48,16,128]{3,2,1,0:T(8,128)S(1)}) custom-call(bf16[4,48,32,128]{3,2,1,0:T(8,128)(2,1)S(1)} %get-tuple-element.14.mid_ref, f32[4,48,16,128]{3,2,1,0:T(8,128)S(1)} %get-tuple-element.15.strip_in_ref, f32[200,64,128]{2,1,0:T(8,128)S(1)} %get-tuple-element.16.pad_ref, ...), custom_call_target="tpu_custom_call", output_to_operand_aliasing={{1}: (1, {})} | custom-call | tf_op jit(solution)/shard_map/edge/pallas_call | solution.py:517
where the time goes:
time: 15.2 us; the launch traced here: 15 us
  Pallas kernels  15 us (99%)
    pallas_call x1, Pallas kernels, per_device(): pl.pallas_call(functools.partial(inner_kernel, sizes), out_shape=(pltpu.V...  12.3 us
    pallas_call x1, Pallas kernels, per_device(): pl.pallas_call(edge_kernel, out_shape=(jax.ShapeDtypeStruct(cells.shape,...  2.73 us

commit v1 on v0

--- a/solution.py
+++ b/solution.py
@@ -29,9 +29,8 @@
     return lambda a, b: pad_ref[line + a, pl.ds(OFF - 1 + b, side), :]
 
 
-def col_lines(flat_pad, side, width, tile, col):
-    first = tile * (side + 2) * width + OFF - 1 + col
-    return lambda a, b: flat_pad[pl.ds(first + a * width + b, side, stride=width), :]
+def col_lines(col_ref, side, tile, n):
+    return lambda a, b: col_ref[tile, n, 2 - b if n else b, pl.ds(OFF - 1 + a, side), :]
 
 
 def conv(dw_ref, dw_bias_ref, side, segments, dst):
@@ -132,12 +131,15 @@
     mid_ref,
     strip_ref,
     pad_ref,
+    col_ref,
     w_aug_ref,
     w_fin_ref,
     dw_ref,
     dw_bias_ref,
     bias_ref,
-    cells_buf,
+    mid_buf,
+    side_buf,
+    cap_buf,
     rims_ref,
     recv_ref,
     send_buf,
@@ -153,13 +155,15 @@
     b_out_ref,
     scale_ref,
     load_sem,
+    cap_sem,
+    side_sem,
     table_sem,
     weight_sem,
     send_sem,
     recv_sem,
 ):
     tile_devices, hidden_devices = sizes
-    tiles, side, _, channels = cells_buf.shape
+    tiles, side, _, channels = cells_ref.shape
     edges = 4 * tiles
     width = side + 2 * OFF
     devices = tile_devices * hidden_devices
@@ -170,13 +174,27 @@
 
     right = lax.rem(me + 1, devices)
     left = lax.rem(me + devices - 1, devices)
-    loads = [
-        pltpu.make_async_copy(cells_ref.at[t], cells_buf.at[t], load_sem.at[t])
-        for t in range(tiles)
-    ]
     tables = [
         pltpu.make_async_copy(src, dst, table_sem.at[n])
         for n, (src, dst) in enumerate(((partner_hbm, partner_ref), (flip_hbm, flip_ref)))
+    ]
+    caps = [
+        pltpu.make_async_copy(cells_ref.at[t, row], cap_buf.at[t, n], cap_sem.at[t, n])
+        for t in range(tiles)
+        for n, row in enumerate((0, side - 1))
+    ]
+    borders = [
+        pltpu.make_async_copy(
+            cells_ref.at[t, :, pl.ds(col, OFF)], side_buf.at[t, n], side_sem.at[t, n]
+        )
+        for t in range(tiles)
+        for n, col in enumerate((0, side - OFF))
+    ]
+    mids = [
+        pltpu.make_async_copy(
+            cells_ref.at[t, :, pl.ds(OFF, side - 2 * OFF)], mid_buf.at[t], load_sem.at[t]
+        )
+        for t in range(tiles)
     ]
     weights = [
         pltpu.make_async_copy(src, dst, weight_sem.at[n])
@@ -194,7 +212,7 @@
             )
         )
     ]
-    for copy in tables + weights[:3] + loads[:1] + weights[3:] + loads[1:]:
+    for copy in tables + caps + borders + weights + mids:
         copy.start()
     barrier = pltpu.get_barrier_semaphore()
     for neighbour in (left, right):
@@ -202,6 +220,62 @@
 
     fill_ones(buf_a)
     fill_ones(buf_b)
+    for copy in tables:
+        copy.wait()
+    partners = [partner_ref[e // 4, e % 4] for e in range(edges)]
+    local = [jnp.int32(e) for e in range(edges)]
+    going = []
+    for device in (right, left):
+        going += last_flagged([owned(p, device, edges)[0] for p in partners], local)
+
+    def one_hot(found):
+        return jnp.where(found, 1.0, 0.0).astype(jnp.bfloat16)
+
+    r_id = lax.broadcasted_iota(jnp.int32, (side, side), 0)
+    c_id = lax.broadcasted_iota(jnp.int32, (side, side), 1)
+    along, against = c_id - r_id, c_id + r_id - (side - 1)
+    r_id = lax.broadcasted_iota(jnp.int32, (side, side * OFF), 0)
+    c_id = lax.broadcasted_iota(jnp.int32, (side, side * OFF), 1)
+    far_along, far_against = c_id - OFF * r_id, c_id + OFF * r_id - OFF * (side - 1)
+    for copy in caps + borders:
+        copy.wait()
+    for t in range(tiles):
+        for s in range(4):
+            flip = flip_ref[t, s] == 1
+            if s % 2 == 0:
+                order = one_hot(jnp.where(flip, against, along) == 0)
+                source = cap_buf[t, s // 2]
+            else:
+                n = 1 - s // 2
+                order = one_hot(jnp.where(flip, far_against, far_along) == n * (OFF - 1))
+                source = side_buf[t, n].reshape(side * OFF, channels)
+            rims_ref[4 * t + s] = jnp.dot(
+                order, source, preferred_element_type=jnp.float32
+            ).astype(jnp.bfloat16)
+    for k in range(2 * CROSS):
+        send_buf[k] = rims_ref[going[k]]
+
+    sends = [
+        pltpu.make_async_remote_copy(
+            src_ref=send_buf.at[pl.ds(side_id * CROSS, CROSS)],
+            dst_ref=recv_ref.at[pl.ds(side_id * CROSS, CROSS)],
+            send_sem=send_sem.at[side_id],
+            recv_sem=recv_sem.at[side_id],
+            device_id=at(target),
+            device_id_type=MESH,
+        )
+        for side_id, target in ((0, right), (1, left))
+    ]
+
+    def send():
+        pl.semaphore_wait(barrier, 2)
+        for copy in sends:
+            copy.start()
+
+    @pl.when(me == devices - 1)
+    def _():
+        send()
+
     for copy in weights:
         copy.wait()
     fold_weights(
@@ -216,46 +290,22 @@
         w_fin_ref,
         bias_ref,
     )
-    for copy in tables:
-        copy.wait()
-    partners = [partner_ref[e // 4, e % 4] for e in range(edges)]
-    local = [jnp.int32(e) for e in range(edges)]
-    going = []
-    for device in (right, left):
-        going += last_flagged([owned(p, device, edges)[0] for p in partners], local)
-
-    flat_pad = pad_ref.reshape(tiles * (side + 2) * width, channels)
     for t in range(tiles):
-        loads[t].wait()
-        top = t * (side + 2)
-        pad_ref[pl.ds(top + 1, side), pl.ds(OFF, side), :] = cells_buf[t].astype(jnp.float32)
-        first = (top + 1) * width + OFF
-        mine = 4 * t
-        rims_ref[mine] = cells_buf[t, 0]
-        rims_ref[mine + 2] = cells_buf[t, side - 1]
-        east = flat_pad[pl.ds(first + side - 1, side, stride=width), :]
-        rims_ref[mine + 1] = east.astype(jnp.bfloat16)
-        west = flat_pad[pl.ds(first, side, stride=width), :]
-        rims_ref[mine + 3] = west.astype(jnp.bfloat16)
-    for k in range(2 * CROSS):
-        send_buf[k] = rims_ref[going[k]]
-
-    sends = [
-        pltpu.make_async_remote_copy(
-            src_ref=send_buf.at[pl.ds(side_id * CROSS, CROSS)],
-            dst_ref=recv_ref.at[pl.ds(side_id * CROSS, CROSS)],
-            send_sem=send_sem.at[side_id],
-            recv_sem=recv_sem.at[side_id],
-            device_id=at(target),
-            device_id_type=MESH,
-        )
-        for side_id, target in ((0, right), (1, left))
-    ]
-
-    def send():
-        pl.semaphore_wait(barrier, 2)
-        for copy in sends:
-            copy.start()
+        rows = pl.ds(t * (side + 2) + 1, side)
+        for n in range(2):
+            line = side_buf[t, n]
+            pad_ref[rows, pl.ds(OFF + n * (side - OFF), OFF), :] = line.astype(jnp.float32)
+            for k in range(2):
+                order = one_hot(far_along == (OFF - 1 - k if n else k))
+                col_ref[t, n, k + 1, pl.ds(OFF, side), :] = jnp.dot(
+                    order,
+                    line.reshape(side * OFF, channels),
+                    preferred_element_type=jnp.float32,
+                )
+    for t in range(tiles):
+        mids[t].wait()
+        rows = pl.ds(t * (side + 2) + 1, side)
+        pad_ref[rows, pl.ds(2 * OFF, side - 2 * OFF), :] = mid_buf[t].astype(jnp.float32)
 
     inner_rows = side - 2
 
@@ -289,7 +339,7 @@
     bufs = (buf_a, buf_b)
     do_conv(0, buf_a)
     rounds = (chunks - 1) // UNROLL
-    turn = jnp.where(me == 0, rounds - 1, jnp.where(me == devices - 1, 0, min(2, rounds - 1)))
+    turn = jnp.where(me == 0, rounds - 1, jnp.where(me == devices - 1, rounds, min(2, rounds - 1)))
 
     @pl.loop(0, rounds)
     def _(i):
@@ -312,8 +362,6 @@
     next_flags, next_local = zip(*[owned(p, right, edges) for p in partners])
     prev_list = last_flagged(prev_flags, prev_local)
     next_list = last_flagged(next_flags, next_local)
-    r_id = lax.broadcasted_iota(jnp.int32, (side, side), 0)
-    c_id = lax.broadcasted_iota(jnp.int32, (side, side), 1)
     for t in range(tiles):
         lines = []
         for s in range(4):
@@ -328,27 +376,27 @@
             own_edge = jnp.clip(jnp.where(crosses, 0, partners[e] - me * edges), 0, edges - 1)
             received = recv_ref[jnp.clip(jnp.where(crosses, slot, 0), 0, 2 * CROSS - 1)]
             line = jnp.where(crosses, received, rims_ref[own_edge])
-            target = jnp.where(flip_ref[t, s] == 1, side - 1 - r_id, r_id)
-            order = jnp.where(c_id == target, 1.0, 0.0).astype(jnp.bfloat16)
-            lines.append(jnp.dot(order, line, preferred_element_type=jnp.float32))
+            lines.append(line.astype(jnp.float32))
         north, east, south, west = lines
         top = t * (side + 2)
         end = top + side + 1
         pad_ref[top, pl.ds(OFF, side), :] = north
         pad_ref[end, pl.ds(OFF, side), :] = south
-        first = (top + 1) * width + OFF
-        flat_pad[pl.ds(first - 1, side, stride=width), :] = west
-        flat_pad[pl.ds(first + side, side, stride=width), :] = east
-        pad_ref[top, OFF - 1 : OFF, :] = 0.5 * (north[:1] + west[:1])
-        pad_ref[top, OFF + side : OFF + side + 1, :] = 0.5 * (north[-1:] + east[:1])
-        pad_ref[end, OFF - 1 : OFF, :] = 0.5 * (south[:1] + west[-1:])
-        pad_ref[end, OFF + side : OFF + side + 1, :] = 0.5 * (south[-1:] + east[-1:])
+        for n, line in enumerate((west, east)):
+            col_ref[t, n, 0, pl.ds(OFF, side), :] = line
+            inner = side - 1 if n else 0
+            outer = pl.ds(OFF + side if n else OFF - 1, 1)
+            pad_ref[top, outer, :] = 0.5 * (north[inner : inner + 1] + line[:1])
+            pad_ref[end, outer, :] = 0.5 * (south[inner : inner + 1] + line[-1:])
+            for row in (0, 1, side - 2, side - 1):
+                pad_ref[top + 1 + row, outer, :] = line[row : row + 1]
 
 
 def edge_kernel(
     mid_ref,
     strip_in_ref,
     pad_ref,
+    col_ref,
     w_aug_ref,
     w_fin_ref,
     dw_ref,
@@ -365,7 +413,6 @@
     side_sem,
 ):
     tiles, side, _, channels = out_hbm.shape
-    width = side + 2 * OFF
     mid_copies = [
         pltpu.make_async_copy(
             mid_ref.at[t, pl.ds(1, side - 2)],
@@ -378,7 +425,6 @@
         copy.start()
     fill_ones(buf_a)
     fill_ones(buf_b)
-    flat_pad = pad_ref.reshape(tiles * (side + 2) * width, channels)
     flat_strip = strip_ref.reshape(tiles * side * 2 * OFF, channels)
 
     def put_cap(tile, n):
@@ -399,8 +445,8 @@
         return [
             (row_lines(pad_ref, side, tile, 0), put_cap(tile, 0)),
             (row_lines(pad_ref, side, tile, side - 1), put_cap(tile, 1)),
-            (col_lines(flat_pad, side, width, tile, 0), put_side(tile, 0)),
-            (col_lines(flat_pad, side, width, tile, side - 1), put_side(tile, 1)),
+            (col_lines(col_ref, side, tile, 0), put_side(tile, 0)),
+            (col_lines(col_ref, side, tile, 1), put_side(tile, 1)),
         ]
 
     groups = [
@@ -480,6 +526,7 @@
             pltpu.VMEM((tiles, side, side - 2 * OFF, channels), jnp.bfloat16),
             pltpu.VMEM(strip_shape, jnp.float32),
             pltpu.VMEM(pad_shape, jnp.float32),
+            pltpu.VMEM((tiles, 2, 3, side + 2 * OFF, channels), jnp.float32),
             pltpu.VMEM((2 * channels, hidden), jnp.bfloat16),
             pltpu.VMEM((hidden, channels), jnp.bfloat16),
             pltpu.VMEM(dw_weight.shape, jnp.float32),
@@ -487,9 +534,11 @@
             vector,
         ),
         in_specs=[anywhere] * len(operands),
-        out_specs=(vmem,) * 8,
+        out_specs=(vmem,) * 9,
         scratch_shapes=[
-            pltpu.VMEM(cells.shape, jnp.bfloat16),
+            pltpu.VMEM((tiles, side, side - 2 * OFF, channels), jnp.bfloat16),
+            pltpu.VMEM((tiles, 2, side, OFF, channels), jnp.bfloat16),
+            pltpu.VMEM((tiles, 2, side, channels), jnp.bfloat16),
             pltpu.VMEM((edges, side, channels), jnp.bfloat16),
             pltpu.VMEM((2 * CROSS, side, channels), jnp.bfloat16),
             pltpu.VMEM((2 * CROSS, side, channels), jnp.bfloat16),
@@ -504,6 +553,8 @@
             vector,
             vector,
             pltpu.SemaphoreType.DMA((tiles,)),
+            pltpu.SemaphoreType.DMA((tiles, 2)),
+            pltpu.SemaphoreType.DMA((tiles, 2)),
             pltpu.SemaphoreType.DMA((2,)),
             pltpu.SemaphoreType.DMA((9,)),
             pltpu.SemaphoreType.DMA((2,)),
@@ -520,7 +571,7 @@
             jax.ShapeDtypeStruct(cells.shape, jnp.bfloat16),
             pltpu.VMEM(strip_shape, jnp.float32),
         ),
-        in_specs=[vmem] * 8,
+        in_specs=[vmem] * 9,
         out_specs=(anywhere, vmem),
         input_output_aliases={1: 1},
         scratch_shapes=[

time: 15.2 us -> 15 us (0.987)
  Pallas kernels: 15 us -> 14.8 us
    pallas_call x1, Pallas kernels: 2.73 us -> 2.03 us  [per_device(): pl.pallas_call(edge_kernel, out_shape=(jax.ShapeDtypeStruct(cells.shape,...]
    pallas_call x1, Pallas kernels: 12.3 us -> 12.8 us  [per_device(): pl.pallas_call(functools.partial(inner_kernel, sizes), out_shape=(pltpu.V...]
where the time goes in v1:
time: 15 us; the launch traced here: 14.8 us
  Pallas kernels  14.8 us (99%)
    pallas_call x1, Pallas kernels, per_device(): pl.pallas_call(functools.partial(inner_kernel, sizes), out_shape=(pltpu.V...  12.8 us
    pallas_call x1, Pallas kernels, per_device(): pl.pallas_call(edge_kernel, out_shape=(jax.ShapeDtypeStruct(cells.shape,...  2.03 us

profile of v1, /device:TPU:0, one launch (start us, length us, event | category | flops | bytes accessed | tf_op | source)
XLA Modules:
  0.0 14.8 jit_solution(9683874737824273621)
XLA Ops:
  0.0 12.8 %inner.1 = (bf16[4,48,32,128]{3,2,1,0:T(8,128)(2,1)S(1)}, f32[4,48,16,128]{3,2,1,0:T(8,128)S(1)}, f32[200,64,128]{2,1,0:T(8,128)S(1)}, f32[4,2,3,64,128]{4,3,2,1...) custom-call(bf16[4,48,48,128]{3,2,1,0:T(8,128)(2,1)} %cells_ref.1, ...), custom_call_target="tpu_custom_call" | custom-call | tf_op jit(solution)/shard_map/inner/pallas_call | solution.py:523
  12.8 2.0 %edge.1 = (bf16[4,48,48,128]{3,2,1,0:T(8,128)(2,1)}, f32[4,48,16,128]{3,2,1,0:T(8,128)S(1)}) custom-call(bf16[4,48,32,128]{3,2,1,0:T(8,128)(2,1)S(1)} %get-tuple-element.15.mid_ref, f32[4,48,16,128]{3,2,1,0:T(8,128)S(1)} %get-tuple-element.16.strip_in_ref, f32[200,64,128]{2,1,0:T(8,128)S(1)} %get-tuple-element.17.pad_ref, ...), custom_call_target="tpu_custom_call", output_to_operand_aliasing={{1}: (1, {})} | custom-call | tf_op jit(solution)/shard_map/edge/pallas_call | solution.py:568

commit v2 on v1

--- a/solution.py
+++ b/solution.py
@@ -10,7 +10,7 @@
 AXES = ("tile", "hidden")
 OFF = 8
 ROWS = 8
-UNROLL = 2
+UNROLL = 4
 CROSS = 4
 GRANT = 40 * 1024 * 1024
 MESH = pl.DeviceIdType.MESH
@@ -339,7 +339,7 @@
     bufs = (buf_a, buf_b)
     do_conv(0, buf_a)
     rounds = (chunks - 1) // UNROLL
-    turn = jnp.where(me == 0, rounds - 1, jnp.where(me == devices - 1, rounds, min(2, rounds - 1)))
+    turn = jnp.where(me == 0, rounds - 1, jnp.where(me == devices - 1, rounds, min(1, rounds - 1)))
 
     @pl.loop(0, rounds)
     def _(i):

time: 15 us -> 13.8 us (0.920)
  Pallas kernels: 14.8 us -> 13.6 us
    pallas_call x1, Pallas kernels: 12.8 us -> 11.6 us  [per_device(): pl.pallas_call(functools.partial(inner_kernel, sizes), out_shape=(pltpu.V...]
where the time goes in v2:
time: 13.8 us; the launch traced here: 13.6 us
  Pallas kernels  13.6 us (99%)
    pallas_call x1, Pallas kernels, per_device(): pl.pallas_call(functools.partial(inner_kernel, sizes), out_shape=(pltpu.V...  11.6 us
    pallas_call x1, Pallas kernels, per_device(): pl.pallas_call(edge_kernel, out_shape=(jax.ShapeDtypeStruct(cells.shape,...  2.03 us

profile of v2, /device:TPU:0, one launch (start us, length us, event | category | flops | bytes accessed | tf_op | source)
XLA Modules:
  0.0 13.6 jit_solution(15941025969952758785)
XLA Ops:
  0.0 11.6 %inner.1 = (bf16[4,48,32,128]{3,2,1,0:T(8,128)(2,1)S(1)}, f32[4,48,16,128]{3,2,1,0:T(8,128)S(1)}, f32[200,64,128]{2,1,0:T(8,128)S(1)}, f32[4,2,3,64,128]{4,3,2,1...) custom-call(bf16[4,48,48,128]{3,2,1,0:T(8,128)(2,1)} %cells_ref.1, ...), custom_call_target="tpu_custom_call" | custom-call | tf_op jit(solution)/shard_map/inner/pallas_call | solution.py:523
  11.6 2.0 %edge.1 = (bf16[4,48,48,128]{3,2,1,0:T(8,128)(2,1)}, f32[4,48,16,128]{3,2,1,0:T(8,128)S(1)}) custom-call(bf16[4,48,32,128]{3,2,1,0:T(8,128)(2,1)S(1)} %get-tuple-element.15.mid_ref, f32[4,48,16,128]{3,2,1,0:T(8,128)S(1)} %get-tuple-element.16.strip_in_ref, f32[200,64,128]{2,1,0:T(8,128)S(1)} %get-tuple-element.17.pad_ref, ...), custom_call_target="tpu_custom_call", output_to_operand_aliasing={{1}: (1, {})} | custom-call | tf_op jit(solution)/shard_map/edge/pallas_call | solution.py:568

commit v3 on v0

--- a/solution.py
+++ b/solution.py
@@ -10,7 +10,7 @@
 AXES = ("tile", "hidden")
 OFF = 8
 ROWS = 8
-UNROLL = 2
+UNROLL = 6
 CROSS = 4
 GRANT = 40 * 1024 * 1024
 MESH = pl.DeviceIdType.MESH
@@ -24,14 +24,18 @@
     return tile
 
 
-def row_lines(pad_ref, side, tile, row):
-    line = tile * (side + 2) + row
-    return lambda a, b: pad_ref[line + a, pl.ds(OFF - 1 + b, side), :]
-
-
-def col_lines(flat_pad, side, width, tile, col):
-    first = tile * (side + 2) * width + OFF - 1 + col
-    return lambda a, b: flat_pad[pl.ds(first + a * width + b, side, stride=width), :]
+def rim_lines(line_ref, length, tile, s):
+    def load(a, b):
+        across, along = (a, b) if s % 2 == 0 else (b, a)
+        return line_ref[tile, s, across if s in (0, 3) else 2 - across, pl.ds(OFF - 1 + along, length), :]
+
+    return load
+
+
+def normed(total, eps):
+    center = total - jnp.mean(total, axis=-1, keepdims=True)
+    spread = jnp.sum(center * center, axis=-1, keepdims=True)
+    return (center * lax.rsqrt(spread + eps)).astype(jnp.bfloat16)
 
 
 def conv(dw_ref, dw_bias_ref, side, segments, dst):
@@ -41,10 +45,38 @@
         for a in range(3):
             for b in range(3):
                 total = total + dw_ref[3 * a + b : 3 * a + b + 1] * load(a, b)
-        center = total - jnp.mean(total, axis=-1, keepdims=True)
-        spread = jnp.sum(center * center, axis=-1, keepdims=True)
-        value = center * lax.rsqrt(spread + 1e-06 * channels)
-        dst[n * side : (n + 1) * side, 0:channels] = value.astype(jnp.bfloat16)
+        dst[n * side : (n + 1) * side, 0:channels] = normed(total, 1e-06 * channels)
+
+
+def whole_line(cells_buf, tile, row):
+    side, step = cells_buf.shape[2], 2 * OFF
+    return jnp.concatenate(
+        [cells_buf[tile, row, n : n + step] for n in range(0, side, step)], axis=0
+    )
+
+
+def conv_rows(dw_ref, dw_bias_ref, cells_buf, shift_ref, rows, dst):
+    side, channels = cells_buf.shape[2:]
+    taps = [
+        jnp.broadcast_to(dw_ref[k : k + 1], (side, channels)).astype(jnp.bfloat16)
+        for k in range(9)
+    ]
+    for n, (tile, row) in enumerate(rows):
+        lines = [
+            whole_line(cells_buf, tile, row - 1 + a) for a in range(3)
+        ]
+        sums = []
+        for b in range(3):
+            part = taps[b] * lines[0]
+            for a in range(1, 3):
+                part = part + taps[3 * a + b] * lines[a]
+            sums.append(part.astype(jnp.float32))
+        shift_ref[n, 0, pl.ds(OFF, side), :] = sums[0]
+        shift_ref[n, 1, pl.ds(OFF, side), :] = sums[2]
+        total = (sums[1] + dw_bias_ref[...]) + (
+            shift_ref[n, 0, pl.ds(OFF - 1, side), :] + shift_ref[n, 1, pl.ds(OFF + 1, side), :]
+        )
+        dst[n * side : (n + 1) * side, 0:channels] = normed(total, 1e-06 * channels)
 
 
 def mlp(w_aug_ref, w_fin_ref, bias_ref, side, segments, src):
@@ -53,7 +85,7 @@
     act = z * (lax.erf(z) + jnp.bfloat16(1))
     mixed = jnp.dot(act, w_fin_ref[...], preferred_element_type=jnp.float32)
     for n, (load, store) in enumerate(segments):
-        store(load(1, 1) + (mixed[n * side : (n + 1) * side] + bias_ref[...]))
+        store(load(1, 1).astype(jnp.float32) + (mixed[n * side : (n + 1) * side] + bias_ref[...]))
 
 
 def fill_ones(buf):
@@ -131,18 +163,21 @@
     scale_hbm,
     mid_ref,
     strip_ref,
-    pad_ref,
+    line_ref,
     w_aug_ref,
     w_fin_ref,
     dw_ref,
     dw_bias_ref,
     bias_ref,
     cells_buf,
+    side_buf,
+    cap_buf,
     rims_ref,
     recv_ref,
     send_buf,
     buf_a,
     buf_b,
+    shift_ref,
     partner_ref,
     flip_ref,
     gain_ref,
@@ -153,15 +188,16 @@
     b_out_ref,
     scale_ref,
     load_sem,
+    cap_sem,
+    side_sem,
     table_sem,
     weight_sem,
     send_sem,
     recv_sem,
 ):
     tile_devices, hidden_devices = sizes
-    tiles, side, _, channels = cells_buf.shape
+    tiles, side, _, channels = cells_ref.shape
     edges = 4 * tiles
-    width = side + 2 * OFF
     devices = tile_devices * hidden_devices
     me = lax.axis_index("tile") * hidden_devices + lax.axis_index("hidden")
 
@@ -170,13 +206,25 @@
 
     right = lax.rem(me + 1, devices)
     left = lax.rem(me + devices - 1, devices)
+    tables = [
+        pltpu.make_async_copy(src, dst, table_sem.at[n])
+        for n, (src, dst) in enumerate(((partner_hbm, partner_ref), (flip_hbm, flip_ref)))
+    ]
+    caps = [
+        pltpu.make_async_copy(cells_ref.at[t, row], cap_buf.at[t, n], cap_sem.at[t, n])
+        for t in range(tiles)
+        for n, row in enumerate((0, side - 1))
+    ]
+    borders = [
+        pltpu.make_async_copy(
+            cells_ref.at[t, :, pl.ds(col, OFF)], side_buf.at[t, n], side_sem.at[t, n]
+        )
+        for t in range(tiles)
+        for n, col in enumerate((0, side - OFF))
+    ]
     loads = [
         pltpu.make_async_copy(cells_ref.at[t], cells_buf.at[t], load_sem.at[t])
         for t in range(tiles)
-    ]
-    tables = [
-        pltpu.make_async_copy(src, dst, table_sem.at[n])
-        for n, (src, dst) in enumerate(((partner_hbm, partner_ref), (flip_hbm, flip_ref)))
     ]
     weights = [
         pltpu.make_async_copy(src, dst, weight_sem.at[n])
@@ -194,7 +242,7 @@
             )
         )
     ]
-    for copy in tables + weights[:3] + loads[:1] + weights[3:] + loads[1:]:
+    for copy in tables + weights + caps + borders + loads:
         copy.start()
     barrier = pltpu.get_barrier_semaphore()
     for neighbour in (left, right):
@@ -202,6 +250,8 @@
 
     fill_ones(buf_a)
     fill_ones(buf_b)
+    for copy in tables:
+        copy.wait()
     for copy in weights:
         copy.wait()
     fold_weights(
@@ -216,7 +266,22 @@
         w_fin_ref,
         bias_ref,
     )
-    for copy in tables:
+
+    def one_hot(found):
+        return jnp.where(found, 1.0, 0.0).astype(jnp.bfloat16)
+
+    r_id = lax.broadcasted_iota(jnp.int32, (side, side), 0)
+    c_id = lax.broadcasted_iota(jnp.int32, (side, side), 1)
+    backward = one_hot(c_id + r_id == side - 1)
+    r_id = lax.broadcasted_iota(jnp.int32, (side, side * OFF), 0)
+    c_id = lax.broadcasted_iota(jnp.int32, (side, side * OFF), 1)
+    picks = [
+        jnp.concatenate(
+            [one_hot(c_id - OFF * r_id == (OFF - 1 - k if n else k)) for k in range(2)], axis=0
+        )
+        for n in range(2)
+    ]
+    for copy in caps + borders:
         copy.wait()
     partners = [partner_ref[e // 4, e % 4] for e in range(edges)]
     local = [jnp.int32(e) for e in range(edges)]
@@ -224,19 +289,48 @@
     for device in (right, left):
         going += last_flagged([owned(p, device, edges)[0] for p in partners], local)
 
-    flat_pad = pad_ref.reshape(tiles * (side + 2) * width, channels)
-    for t in range(tiles):
-        loads[t].wait()
-        top = t * (side + 2)
-        pad_ref[pl.ds(top + 1, side), pl.ds(OFF, side), :] = cells_buf[t].astype(jnp.float32)
-        first = (top + 1) * width + OFF
-        mine = 4 * t
-        rims_ref[mine] = cells_buf[t, 0]
-        rims_ref[mine + 2] = cells_buf[t, side - 1]
-        east = flat_pad[pl.ds(first + side - 1, side, stride=width), :]
-        rims_ref[mine + 1] = east.astype(jnp.bfloat16)
-        west = flat_pad[pl.ds(first, side, stride=width), :]
-        rims_ref[mine + 3] = west.astype(jnp.bfloat16)
+    prev_flags, prev_local = zip(*[owned(p, left, edges) for p in partners])
+    next_flags, next_local = zip(*[owned(p, right, edges) for p in partners])
+    prev_list = last_flagged(prev_flags, prev_local)
+    next_list = last_flagged(next_flags, next_local)
+    halo_source = []
+    for e in range(edges):
+        slot = jnp.where(
+            prev_flags[e],
+            above(prev_list, prev_local[e]),
+            CROSS + above(next_list, next_local[e]),
+        )
+        crosses = prev_flags[e] | next_flags[e]
+        own_edge = jnp.clip(jnp.where(crosses, 0, partners[e] - me * edges), 0, edges - 1)
+        slot = jnp.clip(jnp.where(crosses, slot, 0), 0, 2 * CROSS - 1)
+        halo_source.append((crosses, slot, own_edge))
+
+    lines = {}
+    for n, s in enumerate((3, 1)):
+        both = jnp.dot(
+            picks[n],
+            jnp.concatenate(
+                [side_buf[t, n].reshape(side * OFF, channels) for t in range(tiles)], axis=1
+            ),
+            preferred_element_type=jnp.float32,
+        )
+        for t in range(tiles):
+            part = both[:, t * channels : (t + 1) * channels]
+            for k in range(2):
+                line_ref[t, s, k + 1, pl.ds(OFF, side), :] = part[k * side : (k + 1) * side]
+            lines[t, s] = part[:side].astype(jnp.bfloat16)
+            lines[t, 2 * n] = cap_buf[t, n]
+    turned = jnp.dot(
+        backward,
+        jnp.concatenate([lines[e // 4, e % 4] for e in range(edges)], axis=1),
+        preferred_element_type=jnp.float32,
+    ).astype(jnp.bfloat16)
+    for e in range(edges):
+        rims_ref[e] = jnp.where(
+            flip_ref[e // 4, e % 4] == 1,
+            turned[:, e * channels : (e + 1) * channels],
+            lines[e // 4, e % 4],
+        )
     for k in range(2 * CROSS):
         send_buf[k] = rims_ref[going[k]]
 
@@ -257,6 +351,10 @@
         for copy in sends:
             copy.start()
 
+    @pl.when(me == devices - 1)
+    def _():
+        send()
+
     inner_rows = side - 2
 
     def rows_of(chunk):
@@ -267,9 +365,10 @@
             found.append((tile, q - inner_rows * tile + 1))
         return found
 
-    def do_conv(chunk, dst):
-        lines = [row_lines(pad_ref, side, tile, row) for tile, row in rows_of(chunk)]
-        conv(dw_ref, dw_bias_ref, side, lines, dst)
+    def do_conv(chunk, parity):
+        conv_rows(
+            dw_ref, dw_bias_ref, cells_buf, shift_ref.at[parity], rows_of(chunk), bufs[parity]
+        )
 
     def put(tile, row):
         def store(new):
@@ -279,76 +378,78 @@
 
         return store
 
-    def do_mlp(chunk, src):
+    def do_mlp(chunk, parity):
         lines = [
-            (row_lines(pad_ref, side, tile, row), put(tile, row)) for tile, row in rows_of(chunk)
+            (lambda a, b, tile=tile, row=row: whole_line(cells_buf, tile, row), put(tile, row))
+            for tile, row in rows_of(chunk)
         ]
-        mlp(w_aug_ref, w_fin_ref, bias_ref, side, lines, src)
+        mlp(w_aug_ref, w_fin_ref, bias_ref, side, lines, bufs[parity])
 
     chunks = tiles * inner_rows // ROWS
     bufs = (buf_a, buf_b)
-    do_conv(0, buf_a)
     rounds = (chunks - 1) // UNROLL
-    turn = jnp.where(me == 0, rounds - 1, jnp.where(me == devices - 1, 0, min(2, rounds - 1)))
+    at_once = tiles if rounds < 2 or ROWS * (UNROLL + 1) > inner_rows else 1
+    for copy in loads[:at_once]:
+        copy.wait()
+    do_conv(0, 0)
+    turn = jnp.where((me == 0) | (me == devices - 1), rounds, min(1, rounds - 1))
 
     @pl.loop(0, rounds)
     def _(i):
+        if at_once < tiles:
+
+            @pl.when(i == 1)
+            def _():
+                for copy in loads[at_once:]:
+                    copy.wait()
+
         @pl.when(i == turn)
         def _():
             send()
 
         for u in range(UNROLL):
-            do_mlp(UNROLL * i + u, bufs[u % 2])
-            do_conv(UNROLL * i + u + 1, bufs[(u + 1) % 2])
-
+            do_mlp(UNROLL * i + u, u % 2)
+            do_conv(UNROLL * i + u + 1, (u + 1) % 2)
+
+    @pl.when(me == 0)
+    def _():
+        send()
+
+    for t in range(tiles):
+        for s, rows in ((0, (0, 1)), (2, (side - 1, side - 2))):
+            for k, row in enumerate(rows):
+                line_ref[t, s, k + 1, pl.ds(OFF, side), :] = cells_buf[t, row].astype(jnp.float32)
     for c in range((chunks - 1) // UNROLL * UNROLL, chunks):
-        do_mlp(c, bufs[c % 2])
+        do_mlp(c, c % 2)
         if c + 1 < chunks:
-            do_conv(c + 1, bufs[(c + 1) % 2])
+            do_conv(c + 1, (c + 1) % 2)
     for copy in sends:
         copy.wait()
 
-    prev_flags, prev_local = zip(*[owned(p, left, edges) for p in partners])
-    next_flags, next_local = zip(*[owned(p, right, edges) for p in partners])
-    prev_list = last_flagged(prev_flags, prev_local)
-    next_list = last_flagged(next_flags, next_local)
-    r_id = lax.broadcasted_iota(jnp.int32, (side, side), 0)
-    c_id = lax.broadcasted_iota(jnp.int32, (side, side), 1)
     for t in range(tiles):
         lines = []
-        for s in range(4):
-            e = 4 * t + s
-            is_prev, is_next = prev_flags[e], next_flags[e]
-            slot = jnp.where(
-                is_prev,
-                above(prev_list, prev_local[e]),
-                CROSS + above(next_list, next_local[e]),
-            )
-            crosses = is_prev | is_next
-            own_edge = jnp.clip(jnp.where(crosses, 0, partners[e] - me * edges), 0, edges - 1)
-            received = recv_ref[jnp.clip(jnp.where(crosses, slot, 0), 0, 2 * CROSS - 1)]
-            line = jnp.where(crosses, received, rims_ref[own_edge])
-            target = jnp.where(flip_ref[t, s] == 1, side - 1 - r_id, r_id)
-            order = jnp.where(c_id == target, 1.0, 0.0).astype(jnp.bfloat16)
-            lines.append(jnp.dot(order, line, preferred_element_type=jnp.float32))
-        north, east, south, west = lines
-        top = t * (side + 2)
-        end = top + side + 1
-        pad_ref[top, pl.ds(OFF, side), :] = north
-        pad_ref[end, pl.ds(OFF, side), :] = south
-        first = (top + 1) * width + OFF
-        flat_pad[pl.ds(first - 1, side, stride=width), :] = west
-        flat_pad[pl.ds(first + side, side, stride=width), :] = east
-        pad_ref[top, OFF - 1 : OFF, :] = 0.5 * (north[:1] + west[:1])
-        pad_ref[top, OFF + side : OFF + side + 1, :] = 0.5 * (north[-1:] + east[:1])
-        pad_ref[end, OFF - 1 : OFF, :] = 0.5 * (south[:1] + west[-1:])
-        pad_ref[end, OFF + side : OFF + side + 1, :] = 0.5 * (south[-1:] + east[-1:])
+        for crosses, slot, own_edge in halo_source[4 * t : 4 * t + 4]:
+            line = jnp.where(crosses, recv_ref[slot], rims_ref[own_edge])
+            lines.append(line.astype(jnp.float32))
+        for s, line in enumerate(lines):
+            line_ref[t, s, 0, pl.ds(OFF, side), :] = line
+        for s in (0, 2):
+            for n, line in enumerate((lines[3], lines[1])):
+                end = pl.ds(OFF + side if n else OFF - 1, 1)
+                near = side - 1 if n else 0
+                first = side - 1 if s else 0
+                second = side - 2 if s else 1
+                line_ref[t, s, 0, end, :] = 0.5 * (
+                    lines[s][near : near + 1] + line[first : first + 1]
+                )
+                line_ref[t, s, 1, end, :] = line[first : first + 1]
+                line_ref[t, s, 2, end, :] = line[second : second + 1]
 
 
 def edge_kernel(
     mid_ref,
     strip_in_ref,
-    pad_ref,
+    line_ref,
     w_aug_ref,
     w_fin_ref,
     dw_ref,
@@ -365,7 +466,6 @@
     side_sem,
 ):
     tiles, side, _, channels = out_hbm.shape
-    width = side + 2 * OFF
     mid_copies = [
         pltpu.make_async_copy(
             mid_ref.at[t, pl.ds(1, side - 2)],
@@ -378,7 +478,6 @@
         copy.start()
     fill_ones(buf_a)
     fill_ones(buf_b)
-    flat_pad = pad_ref.reshape(tiles * (side + 2) * width, channels)
     flat_strip = strip_ref.reshape(tiles * side * 2 * OFF, channels)
 
     def put_cap(tile, n):
@@ -397,10 +496,13 @@
 
     def lines_of(tile):
         return [
-            (row_lines(pad_ref, side, tile, 0), put_cap(tile, 0)),
-            (row_lines(pad_ref, side, tile, side - 1), put_cap(tile, 1)),
-            (col_lines(flat_pad, side, width, tile, 0), put_side(tile, 0)),
-            (col_lines(flat_pad, side, width, tile, side - 1), put_side(tile, 1)),
+            (rim_lines(line_ref, side, tile, s), store)
+            for s, store in (
+                (0, put_cap(tile, 0)),
+                (2, put_cap(tile, 1)),
+                (3, put_side(tile, 0)),
+                (1, put_side(tile, 1)),
+            )
         ]
 
     groups = [
@@ -470,7 +572,6 @@
             layer_scale,
         )
     ]
-    pad_shape = (tiles * (side + 2), side + 2 * OFF, channels)
     strip_shape = (tiles, side, 2 * OFF, channels)
     vector = pltpu.VMEM((1, channels), jnp.float32)
     buffers = [pltpu.VMEM((ROWS * side, 2 * channels), jnp.bfloat16)] * 2
@@ -479,7 +580,7 @@
         out_shape=(
             pltpu.VMEM((tiles, side, side - 2 * OFF, channels), jnp.bfloat16),
             pltpu.VMEM(strip_shape, jnp.float32),
-            pltpu.VMEM(pad_shape, jnp.float32),
+            pltpu.VMEM((tiles, 4, 3, side + 2 * OFF, channels), jnp.float32),
             pltpu.VMEM((2 * channels, hidden), jnp.bfloat16),
             pltpu.VMEM((hidden, channels), jnp.bfloat16),
             pltpu.VMEM(dw_weight.shape, jnp.float32),
@@ -490,10 +591,13 @@
         out_specs=(vmem,) * 8,
         scratch_shapes=[
             pltpu.VMEM(cells.shape, jnp.bfloat16),
+            pltpu.VMEM((tiles, 2, side, OFF, channels), jnp.bfloat16),
+            pltpu.VMEM((tiles, 2, side, channels), jnp.bfloat16),
             pltpu.VMEM((edges, side, channels), jnp.bfloat16),
             pltpu.VMEM((2 * CROSS, side, channels), jnp.bfloat16),
             pltpu.VMEM((2 * CROSS, side, channels), jnp.bfloat16),
             *buffers,
+            pltpu.VMEM((2, ROWS, 2, side + 2 * OFF, channels), jnp.float32),
             pltpu.SMEM(tables[0].shape, jnp.int32),
             pltpu.SMEM(tables[1].shape, jnp.int32),
             vector,
@@ -504,6 +608,8 @@
             vector,
             vector,
             pltpu.SemaphoreType.DMA((tiles,)),
+            pltpu.SemaphoreType.DMA((tiles, 2)),
+            pltpu.SemaphoreType.DMA((tiles, 2)),
             pltpu.SemaphoreType.DMA((2,)),
             pltpu.SemaphoreType.DMA((9,)),
             pltpu.SemaphoreType.DMA((2,)),

time: 15.2 us -> 13.5 us (0.89)
  Pallas kernels: 15 us -> 13.3 us
    pallas_call x1, Pallas kernels: 12.3 us -> 11.3 us  [per_device(): pl.pallas_call(functools.partial(inner_kernel, sizes), out_shape=(pltpu.V...]
    pallas_call x1, Pallas kernels: 2.73 us -> 2.08 us  [per_device(): pl.pallas_call(edge_kernel, out_shape=(jax.ShapeDtypeStruct(cells.shape,...]
where the time goes in v3:
time: 13.5 us; the launch traced here: 13.3 us
  Pallas kernels  13.3 us (99%)
    pallas_call x1, Pallas kernels, per_device(): pl.pallas_call(functools.partial(inner_kernel, sizes), out_shape=(pltpu.V...  11.3 us
    pallas_call x1, Pallas kernels, per_device(): pl.pallas_call(edge_kernel, out_shape=(jax.ShapeDtypeStruct(cells.shape,...  2.08 us

profile of v3, /device:TPU:0, one launch (start us, length us, event | category | flops | bytes accessed | tf_op | source)
XLA Modules:
  0.0 13.3 jit_solution(12427934215895760875)
XLA Ops:
  0.0 11.3 %inner.1 = (bf16[4,48,32,128]{3,2,1,0:T(8,128)(2,1)S(1)}, f32[4,48,16,128]{3,2,1,0:T(8,128)S(1)}, f32[4,4,3,64,128]{4,3,2,1,0:T(8,128)S(1)}, bf16[256,512]{1,0:T...) custom-call(bf16[4,48,48,128]{3,2,1,0:T(8,128)(2,1)} %cells_ref.1, ...), custom_call_target="tpu_custom_call" | custom-call | tf_op jit(solution)/shard_map/inner/pallas_call | solution.py:578
  11.3 2.1 %edge.1 = (bf16[4,48,48,128]{3,2,1,0:T(8,128)(2,1)}, f32[4,48,16,128]{3,2,1,0:T(8,128)S(1)}) custom-call(bf16[4,48,32,128]{3,2,1,0:T(8,128)(2,1)S(1)} %get-tuple-element.14.mid_ref, f32[4,48,16,128]{3,2,1,0:T(8,128)S(1)} %get-tuple-element.15.strip_in_ref, f32[4,4,3,64,128]{4,3,2,1,0:T(8,128)S(1)} %get-tuple-element.16.line_ref, ...), custom_call_target="tpu_custom_call", output_to_operand_aliasing={{1}: (1, {})} | custom-call | tf_op jit(solution)/shard_map/edge/pallas_call | solution.py:623

commit v4 on v3

--- a/solution.py
+++ b/solution.py
@@ -10,7 +10,7 @@
 AXES = ("tile", "hidden")
 OFF = 8
 ROWS = 8
-UNROLL = 6
+UNROLL = 8
 CROSS = 4
 GRANT = 40 * 1024 * 1024
 MESH = pl.DeviceIdType.MESH

time: 13.5 us -> 13.2 us (0.978)
  Pallas kernels: 13.3 us -> 13.1 us
    pallas_call x1, Pallas kernels: 11.3 us -> 11 us  [per_device(): pl.pallas_call(functools.partial(inner_kernel, sizes), out_shape=(pltpu.V...]
where the time goes in v4:
time: 13.2 us; the launch traced here: 13.1 us
  Pallas kernels  13.1 us (99%)
    pallas_call x1, Pallas kernels, per_device(): pl.pallas_call(functools.partial(inner_kernel, sizes), out_shape=(pltpu.V...  11 us
    pallas_call x1, Pallas kernels, per_device(): pl.pallas_call(edge_kernel, out_shape=(jax.ShapeDtypeStruct(cells.shape,...  2.07 us

profile of v4, /device:TPU:0, one launch (start us, length us, event | category | flops | bytes accessed | tf_op | source)
XLA Modules:
  0.0 13.1 jit_solution(16304100981080624129)
XLA Ops:
  0.0 11.0 %inner.1 = (bf16[4,48,32,128]{3,2,1,0:T(8,128)(2,1)S(1)}, f32[4,48,16,128]{3,2,1,0:T(8,128)S(1)}, f32[4,4,3,64,128]{4,3,2,1,0:T(8,128)S(1)}, bf16[256,512]{1,0:T...) custom-call(bf16[4,48,48,128]{3,2,1,0:T(8,128)(2,1)} %cells_ref.1, ...), custom_call_target="tpu_custom_call" | custom-call | tf_op jit(solution)/shard_map/inner/pallas_call | solution.py:578
  11.0 2.1 %edge.1 = (bf16[4,48,48,128]{3,2,1,0:T(8,128)(2,1)}, f32[4,48,16,128]{3,2,1,0:T(8,128)S(1)}) custom-call(bf16[4,48,32,128]{3,2,1,0:T(8,128)(2,1)S(1)} %get-tuple-element.14.mid_ref, f32[4,48,16,128]{3,2,1,0:T(8,128)S(1)} %get-tuple-element.15.strip_in_ref, f32[4,4,3,64,128]{4,3,2,1,0:T(8,128)S(1)} %get-tuple-element.16.line_ref, ...), custom_call_target="tpu_custom_call", output_to_operand_aliasing={{1}: (1, {})} | custom-call | tf_op jit(solution)/shard_map/edge/pallas_call | solution.py:623
